TPU v7x, 32 devices: a whole 2x2x4 slice. The times are simulated.
32 devices in a mesh: groups: 2 (over y), visit: 4 (over z), strip: 2 (over x), band: 2 (over core).
Axes of the slice: x: 2, y: 2, z: 4, core: 2. Of those that a mesh axis runs over, the one named last changes fastest.
Arguments:
- images: bfloat16 [2, 128, 128, 256], P('band', ('groups', 'visit'), 'strip'), parts along dimension 1, may hold values from -8 to 8
- mask_bits: int32 [2, 128, 128, 256], P('band', ('groups', 'visit'), 'strip'), parts along dimension 1, may hold values from 0 to 15
- visit_weight: bfloat16 [2, 128], P('band', ('groups', 'visit')), parts along dimension 1, may hold values from 1 to 4
- intersection: int32 [128, 1], P(('groups', 'visit')), parts along dimension 0, may hold values from 0 to 3, as said below
- patch_owner: int32 [8], P('groups'), parts along dimension 0, may hold values from 0 to 3, each once
Outputs:
- coadd_image: bfloat16 [2, 8, 128, 256], P('band', ('groups', 'visit'), 'strip'), parts along dimension 1
- difference: bfloat16 [2, 128, 128, 256], P('band', ('groups', 'visit'), 'strip'), parts along dimension 1
There are 2 independent parts, one for each index of `groups`. A program takes and returns all parts, laid end to end along the dimension named above; each array names one. Nothing has to cross between parts.
Inputs may be any that keep to these rules, and one draw needn't show every extreme that they name: `intersection`: row j names the patch that piece j intersections. The 16 pieces of one visit index intersect 16 // 8 distinct patches, exactly 8 pieces each; one patch is intersected by 8 pieces of every visit index, and every patch is intersected by some piece. `patch_owner`: A permutation of the patches.
All inputs are finite; a program needn't handle non-finite values.
Results may differ from a plain program's by a relative error of at most 0.0071.
Values may be sent and summed in bfloat16 or wider, within the bound.
A program may use at most 64 MiB of HBM per device.

v0:
```python
import functools

import jax
import jax.numpy as jnp
import numpy as np
from jax import lax
from jax.experimental import pallas as pl
from jax.experimental.pallas import tpu as pltpu
from jax.sharding import PartitionSpec as P

BASES = 6
HALF = 9
TILE = 16

basis_rows = (0, 0, 1, 0, 2, 1)
basis_cols = (0, 1, 0, 2, 0, 1)
pairs = tuple((a, c) for a in range(BASES) for c in range(a, BASES))
MESH = pl.DeviceIdType.MESH
F32 = jnp.float32
BF16 = jnp.bfloat16


def kernel_taps():
    offsets = np.arange(2 * HALF + 1).astype(np.float32) - HALF
    gaussian = np.exp(-offsets * offsets / np.float32(18.0))
    centre = np.sum(offsets * offsets * gaussian * gaussian) / np.sum(gaussian * gaussian)
    table = np.stack([gaussian, offsets * gaussian, (offsets * offsets - centre) * gaussian])
    table = table / np.sqrt(np.sum(table * table, axis=1, keepdims=True))
    return table.astype(BF16).astype(np.float32)


def band_matrix(table, lead, trail, displace):
    index = np.arange(trail)[None, :] - np.arange(lead)[:, None] + displace
    inside = (index >= 0) & (index <= 2 * HALF)
    return np.where(inside[None], table[:, np.clip(index, 0, 2 * HALF)], 0.0)


def gather_matrix():
    result = np.zeros((BASES * 8, (len(pairs) + BASES) * TILE), np.float32)
    for n, (a, c) in enumerate(pairs):
        result[a * 8 + c, n * TILE : (n + 1) * TILE] = 1.0
        result[c * 8 + a, n * TILE : (n + 1) * TILE] = 1.0
    for a in range(BASES):
        n = len(pairs) + a
        result[a * 8 + 6, n * TILE : (n + 1) * TILE] = 1.0
    return result


def iota(shape, dim):
    return lax.broadcasted_iota(jnp.int32, shape, dim)


def nn(a, b):
    return jnp.dot(a, b, preferred_element_type=F32)


def nt(a, b, precision=None):
    return lax.dot_general(
        a, b, (((1,), (1,)), ((), ())), preferred_element_type=F32, precision=precision
    )


def kernel(
    visits, strips, distinct,
    images, masks, weight, cross, owner, cross_scalar, across_in, vertical_in, collect_in,
    coadd_out, diff_out,
    image_v, mask_v, across, vertical, collect, use, use_image, sums, send, recv, gath,
    basis, prods, small, small_in, diff_v,
    in_sem, const_sem, out_sem, rs_send, rs_recv, ag_send, ag_recv, halo_send, halo_recv,
    st_send, st_recv,
):
    pieces, rows, cols = images.shape[1:]
    blocks = rows // TILE
    span = pieces * TILE
    me = lax.axis_index("visit")
    strip = lax.axis_index("strip")

    loads = []
    for t in range(blocks):
        piece_rows = pl.ds(t * TILE, TILE)
        loads.append((
            pltpu.make_async_copy(masks.at[0, :, piece_rows, :], mask_v.at[t], in_sem.at[0, t]),
            pltpu.make_async_copy(images.at[0, :, piece_rows, :], image_v.at[t], in_sem.at[1, t]),
        ))
    constants = [
        pltpu.make_async_copy(across_in, across, const_sem.at[0]),
        pltpu.make_async_copy(vertical_in, vertical, const_sem.at[1]),
        pltpu.make_async_copy(collect_in, collect, const_sem.at[2]),
    ]
    for pair in loads:
        for copy in pair:
            copy.start()
    for copy in constants:
        copy.start()

    barrier = pltpu.get_barrier_semaphore()
    above = strip > 0
    below = strip < strips - 1

    def other_visit(k):
        return lax.rem(me + k, visits)

    for k in range(visits):
        for hop in range(strips):
            if k == 0 and hop == 0:
                continue
            target = {"visit": other_visit(k), "strip": lax.rem(strip + hop, strips)}
            pl.semaphore_signal(barrier, inc=1, device_id=target, device_id_type=MESH)

    position = jnp.zeros((pieces, 1), jnp.int32)
    for p in range(visits):
        position = position + jnp.where(cross[...] == p, owner[p], 0)
    one_hot = (position == iota((pieces, 128), 1)).astype(F32).astype(BF16)
    eq = (jnp.right_shift(iota((visits * TILE, 128), 0), 4) == iota((visits * TILE, 128), 1))
    spread = nt(eq.astype(F32).astype(BF16), one_hot)
    spread = (spread * weight[...].astype(F32)).astype(BF16)
    e2 = iota((pieces, span), 0) == jnp.right_shift(iota((pieces, span), 1), 4)
    wide = nn(spread, e2.astype(F32).astype(BF16))
    same = (iota((visits * TILE, span), 0) & (TILE - 1)) == (
        iota((visits * TILE, span), 1) & (TILE - 1)
    )
    adder = jnp.where(same, wide, 0.0).astype(BF16)
    e_rows = jnp.right_shift(iota((span, 128), 0), 4) == iota((span, 128), 1)
    e_rows = e_rows.astype(F32).astype(BF16)
    row_hot = nn(e_rows[:, :pieces], one_hot)

    seats = [owner[cross_scalar[j, 0]] for j in range(pieces)]
    slots = [jnp.int32(0)] * distinct
    rank = jnp.int32(0)
    for q in range(visits):
        present = jnp.int32(0)
        for j in range(pieces):
            present = present | jnp.where(seats[j] == q, 1, 0)
        for d in range(distinct):
            slots[d] = slots[d] + jnp.where((present == 1) & (rank == d), q, 0)
        rank = rank + present

    for t in range(blocks):
        for copy in loads[t]:
            copy.wait()
        usable = ((mask_v[t].reshape(span, cols) & 3) != 3).astype(F32).astype(BF16)
        masked = usable * image_v[t].reshape(span, cols)
        lanes = pl.ds(t * cols, cols)
        use[:, lanes] = usable
        use_image[:, lanes] = masked
        for part, value in enumerate((masked, usable)):
            total = nn(adder, value)
            for q in range(visits):
                block = total[q * TILE : (q + 1) * TILE]
                sums[q, part, pl.ds(t * TILE, TILE), :] = block
                send[q, part, pl.ds(t * TILE, TILE), :] = block.astype(BF16)

    pl.semaphore_wait(barrier, visits * strips - 1)

    copies = []
    for k in range(1, visits):
        copies.append(pltpu.make_async_remote_copy(
            src_ref=send.at[other_visit(k)], dst_ref=recv.at[k - 1],
            send_sem=rs_send.at[k - 1], recv_sem=rs_recv.at[k - 1],
            device_id={"visit": other_visit(k)}, device_id_type=MESH,
        ))
    for copy in copies:
        copy.start()

    @pl.when(jnp.logical_not(above))
    def _():
        gath[:, pl.ds(0, TILE), :] = jnp.zeros((visits, TILE, cols), BF16)

    @pl.when(jnp.logical_not(below))
    def _():
        gath[:, pl.ds(TILE + rows, TILE), :] = jnp.zeros((visits, TILE, cols), BF16)

    numerator = sums[me, 0]
    denominator = sums[me, 1]
    for k in range(1, visits):
        copies[k - 1].wait_recv()
        numerator = numerator + recv[k - 1, 0].astype(F32)
        denominator = denominator + recv[k - 1, 1].astype(F32)
    coadd = (numerator / jnp.maximum(denominator, 1.0)).astype(BF16)
    gath[me, pl.ds(TILE, rows), :] = coadd

    mains = []
    for k in range(1, visits):
        place = gath.at[me, pl.ds(TILE, rows)]
        mains.append(pltpu.make_async_remote_copy(
            src_ref=place, dst_ref=place,
            send_sem=ag_send.at[k - 1], recv_sem=ag_recv.at[k - 1],
            device_id={"visit": other_visit(k)}, device_id_type=MESH,
        ))
    downs, ups = [], []
    for k in range(visits):
        downs.append(pltpu.make_async_remote_copy(
            src_ref=gath.at[me, pl.ds(rows, TILE)], dst_ref=gath.at[me, pl.ds(0, TILE)],
            send_sem=halo_send.at[0, k], recv_sem=halo_recv.at[0, k],
            device_id={"visit": other_visit(k), "strip": lax.rem(strip + 1, strips)},
            device_id_type=MESH,
        ))
        ups.append(pltpu.make_async_remote_copy(
            src_ref=gath.at[me, pl.ds(TILE, TILE)], dst_ref=gath.at[me, pl.ds(TILE + rows, TILE)],
            send_sem=halo_send.at[1, k], recv_sem=halo_recv.at[1, k],
            device_id={"visit": other_visit(k), "strip": lax.rem(strip + strips - 1, strips)},
            device_id_type=MESH,
        ))
    for copy in mains:
        copy.start()

    @pl.when(below)
    def _():
        for copy in downs:
            copy.start()

    @pl.when(above)
    def _():
        for copy in ups:
            copy.start()

    coadd_copy = pltpu.make_async_copy(
        gath.at[me, pl.ds(TILE, rows)], coadd_out.at[0, 0], out_sem.at[0]
    )
    coadd_copy.start()
    for copy in constants:
        copy.wait()
    for copy in mains:
        copy.wait_recv()

    @pl.when(above)
    def _():
        for copy in downs:
            copy.wait_recv()

    @pl.when(below)
    def _():
        for copy in ups:
            copy.wait_recv()

    for d in range(distinct):
        template = gath[slots[d]]
        smooth = nn(vertical[...], template).astype(BF16)
        planes = [None] * BASES
        for c in range(3):
            taken = [a for a in range(BASES) if basis_cols[a] == c]
            product = nn(smooth[: len(taken) * rows], across[c]).astype(BF16)
            for a in taken:
                r = basis_rows[a]
                planes[a] = product[r * rows : (r + 1) * rows]
        for a in range(BASES):
            for t in range(blocks):
                basis[d, pl.ds(a * TILE, TILE), pl.ds(t * cols, cols)] = planes[a][
                    t * TILE : (t + 1) * TILE
                ]
        for n, (a, c) in enumerate(pairs):
            product = planes[a] * planes[c]
            for t in range(blocks):
                prods[d, pl.ds(n * TILE, TILE), pl.ds(t * cols, cols)] = product[
                    t * TILE : (t + 1) * TILE
                ]

    def member(d):
        chosen = jnp.where(iota((span, 128), 1) == slots[d], row_hot, 0.0)
        return jnp.sum(chosen, axis=1, keepdims=True)

    def summed(values):
        return jnp.sum(values.reshape(pieces, TILE, values.shape[1]), axis=1)

    def keep(width):
        return (iota((span, width), 0) & (TILE - 1)) == (iota((span, width), 1) & (TILE - 1))

    wide_n = len(pairs) * TILE
    wide_b = BASES * TILE
    normal = jnp.zeros((pieces, wide_n), F32)
    right = jnp.zeros((pieces, wide_b), F32)
    for d in range(distinct):
        mine = member(d)
        normal = normal + summed(jnp.where(keep(wide_n), nt(use[...], prods[d]), 0.0) * mine)
        right = right + summed(jnp.where(keep(wide_b), nt(use_image[...], basis[d]), 0.0) * mine)
    system = nt(collect[:, :wide_n], normal, lax.Precision.HIGHEST) + nt(
        collect[:, wide_n:], right, lax.Precision.HIGHEST
    )
    small[...] = jnp.concatenate(
        [system, jnp.zeros((BASES * 8, 128 - pieces), F32)], axis=1
    )
    exchanges = []
    for hop in range(1, strips):
        exchanges.append(pltpu.make_async_remote_copy(
            src_ref=small, dst_ref=small_in.at[hop - 1],
            send_sem=st_send.at[hop - 1], recv_sem=st_recv.at[hop - 1],
            device_id={"strip": lax.rem(strip + hop, strips)}, device_id_type=MESH,
        ))
    for copy in exchanges:
        copy.start()
    full = small[...]
    for hop in range(1, strips):
        exchanges[hop - 1].wait_recv()
        full = full + small_in[hop - 1]

    line = iota((8, 128), 0)
    table = [
        full[a * 8 : (a + 1) * 8] + jnp.where(line == a, 1.0, 0.0) for a in range(BASES)
    ]
    for column in range(BASES):
        pivot = table[column] / table[column][column : column + 1]
        for i in range(BASES):
            if i != column:
                table[i] = table[i] - table[i][column : column + 1] * pivot
        table[column] = pivot
    found = jnp.zeros((8, 128), F32)
    for a in range(BASES):
        found = found + jnp.where(line == a, table[a][BASES : BASES + 1], 0.0)
    high = found.astype(BF16).astype(F32)
    low = found - high
    both = jnp.concatenate([high, low], axis=0).astype(BF16)
    by_row = nt(e_rows, both).astype(BF16)
    wide_c = 2 * wide_b
    column = iota((16, wide_c), 1)
    source = jnp.where(
        column < wide_b, jnp.right_shift(column, 4), jnp.right_shift(column - wide_b, 4) + 8
    )
    e3 = (source == iota((16, wide_c), 0)).astype(F32).astype(BF16)
    mixer = jnp.where(keep(wide_c), nn(by_row, e3), 0.0)
    mixers = [(mixer * member(d)).astype(BF16) for d in range(distinct)]
    stores = []
    for t in range(blocks):
        lanes = pl.ds(t * cols, cols)
        fitted = jnp.zeros((span, cols), F32)
        for d in range(distinct):
            planes = basis[d, :, lanes]
            fitted = fitted + nn(mixers[d], jnp.concatenate([planes, planes], axis=0))
        result = (image_v[t].reshape(span, cols).astype(F32) - fitted).astype(BF16)
        diff_v[t] = result.reshape(pieces, TILE, cols)
        copy = pltpu.make_async_copy(
            diff_v.at[t], diff_out.at[0, :, pl.ds(t * TILE, TILE), :], out_sem.at[1 + t]
        )
        copy.start()
        stores.append(copy)

    for copy in copies + mains + exchanges:
        copy.wait_send()

    @pl.when(below)
    def _():
        for copy in downs:
            copy.wait_send()

    @pl.when(above)
    def _():
        for copy in ups:
            copy.wait_send()

    coadd_copy.wait()
    for copy in stores:
        copy.wait()


def body(visits, strips, images, mask_bits, visit_weight, intersection, patch_owner):
    _, pieces, rows, cols = images.shape
    blocks = rows // TILE
    distinct = max(1, patch_owner.shape[0] // 2)
    span = pieces * TILE
    taps = kernel_taps()
    across = jnp.asarray(np.transpose(band_matrix(taps, cols, cols, HALF), (0, 2, 1)), BF16)
    vertical = jnp.asarray(
        band_matrix(taps, rows, rows + 2 * TILE, HALF - TILE).reshape(3 * rows, rows + 2 * TILE),
        BF16,
    )
    collect = jnp.asarray(gather_matrix())
    anywhere = pl.BlockSpec(memory_space=pl.ANY)
    vmem = pl.BlockSpec(memory_space=pltpu.VMEM)
    smem = pl.BlockSpec(memory_space=pltpu.SMEM)
    dma = pltpu.SemaphoreType.DMA
    peers = max(1, visits - 1)
    return pl.pallas_call(
        functools.partial(kernel, visits, strips, distinct),
        out_shape=(
            jax.ShapeDtypeStruct((1, 1, rows, cols), BF16),
            jax.ShapeDtypeStruct(images.shape, BF16),
        ),
        in_specs=[anywhere, anywhere, vmem, vmem, smem, smem, anywhere, anywhere, anywhere],
        out_specs=(anywhere, anywhere),
        scratch_shapes=[
            pltpu.VMEM((blocks, pieces, TILE, cols), BF16),
            pltpu.VMEM((blocks, pieces, TILE, cols), jnp.int32),
            pltpu.VMEM(across.shape, BF16),
            pltpu.VMEM(vertical.shape, BF16),
            pltpu.VMEM(collect.shape, F32),
            pltpu.VMEM((span, blocks * cols), BF16),
            pltpu.VMEM((span, blocks * cols), BF16),
            pltpu.VMEM((visits, 2, rows, cols), F32),
            pltpu.VMEM((visits, 2, rows, cols), BF16),
            pltpu.VMEM((peers, 2, rows, cols), BF16),
            pltpu.VMEM((visits, rows + 2 * TILE, cols), BF16),
            pltpu.VMEM((distinct, BASES * TILE, blocks * cols), BF16),
            pltpu.VMEM((distinct, len(pairs) * TILE, blocks * cols), BF16),
            pltpu.VMEM((BASES * 8, 128), F32),
            pltpu.VMEM((max(1, strips - 1), BASES * 8, 128), F32),
            pltpu.VMEM((blocks, pieces, TILE, cols), BF16),
            dma((2, blocks)),
            dma((3,)),
            dma((1 + blocks,)),
            dma((peers,)),
            dma((peers,)),
            dma((peers,)),
            dma((peers,)),
            dma((2, visits)),
            dma((2, visits)),
            dma((max(1, strips - 1),)),
            dma((max(1, strips - 1),)),
        ],
        compiler_params=pltpu.CompilerParams(
            collective_id=0, has_side_effects=True, vmem_limit_bytes=48 * 1024 * 1024
        ),
        name="coadd_difference",
    )(
        images, mask_bits, visit_weight, intersection, patch_owner, intersection,
        across, vertical, collect,
    )


def solution(mesh):
    in_specs = (
        P("band", ("groups", "visit"), "strip", None),
        P("band", ("groups", "visit"), "strip", None),
        P("band", ("groups", "visit")),
        P(("groups", "visit"), None),
        P("groups"),
    )
    out_specs = (
        P("band", ("groups", "visit"), "strip", None),
        P("band", ("groups", "visit"), "strip", None),
    )
    step = functools.partial(body, mesh.shape["visit"], mesh.shape["strip"])
    return jax.shard_map(step, mesh=mesh, in_specs=in_specs, out_specs=out_specs, check_vma=False)
```

profile of v0, /device:TPU:0, one launch (start us, length us, event | category | flops | bytes accessed | tf_op | source)
XLA Modules:
  0.0 33.4 jit_solution(13058555061754615841)
XLA Ops:
  0.6 0.0 copy-start.6
  0.6 0.0 copy-start.5
  0.7 0.7 %copy.10.cross.cross_scalar = s32[16,1]{1,0:T(8,128)S(1)} copy(s32[16,1]{0,1:T(1,128)} %param.11) | data formatting | bytes 128 | tf_op args[3]
  1.4 0.0 copy-done.6
  1.4 0.0 copy-done.5
  1.4 0.0 copy-start
  1.4 1.2 %copy-done = s32[1,16,64,256]{3,2,1,0:T(8,128)S(1)} copy-done((s32[1,16,64,256]{3,2,1,0:T(8,128)S(1)}, s32[1,16,64,256]{3,2,1,0:T(8,128)}, u32[]{:S(2)}) %copy-start) | copy-done | bytes 1048600
  2.6 0.0 copy-start.1
  2.6 1.0 %copy-done.1 = bf16[1,16,64,256]{3,2,1,0:T(8,128)(2,1)S(1)} copy-done((bf16[1,16,64,256]{3,2,1,0:T(8,128)(2,1)S(1)}, bf16[1,16,64,256]{3,2,1,0:T(8,128)(2,1)}, u32[]{:S(2)}) %copy-start.1) | copy-done | bytes 524312
  3.7 0.0 copy-start.2
  3.7 1.0 %copy-done.2 = bf16[3,256,256]{2,1,0:T(8,128)(2,1)S(1)} copy-done((bf16[3,256,256]{2,1,0:T(8,128)(2,1)S(1)}, bf16[3,256,256]{2,1,0:T(8,128)(2,1)}, u32[]{:S(2)}) %copy-start.2) | copy-done | bytes 393240
  4.7 0.0 copy-start.3
  4.7 0.9 %copy-done.3 = f32[48,432]{1,0:T(8,128)S(1)} copy-done((f32[48,432]{1,0:T(8,128)S(1)}, f32[48,432]{1,0:T(8,128)}, u32[]{:S(2)}) %copy-start.3) | copy-done | bytes 82968
  5.6 0.0 copy-start.4
  5.6 0.8 %copy-done.4 = bf16[192,96]{1,0:T(8,128)(2,1)S(1)} copy-done((bf16[192,96]{1,0:T(8,128)(2,1)S(1)}, bf16[192,96]{1,0:T(8,128)(2,1)}, u32[]{:S(2)}) %copy-start.4) | copy-done | bytes 36888
  6.4 25.6 %coadd_difference.1 = (bf16[1,1,64,256]{3,2,1,0:T(8,128)(2,1)S(1)}, bf16[1,16,64,256]{3,2,1,0:T(8,128)(2,1)S(1)}) custom-call(bf16[1,16,64,256]{3,2,1,0:T(8,128)(2,1)S(1)} %copy-done.1, s32[1,16,64,256]{3,2,1,0:T(8,128)S(1)} %copy-done, bf16[1,16]{1,0:T(2,128)(2,1)S(1)} %copy-done.5, s32[16,1]{1,0:T(8,128)S(1)} %copy.10.cross.cross_scalar, s32[4]{0:T(128)S(1)} %copy-done.6, ...), custom_call_target="tpu_custom_call" | custom-call | tf_op jit(solution)/shard_map/coadd_difference/pallas_call | solution.py:371
  32.0 0.6 %copy.14 = bf16[1,1,64,256]{3,2,1,0:T(8,128)(2,1)} copy(bf16[1,1,64,256]{3,2,1,0:T(8,128)(2,1)S(1)} %get-tuple-element.4) | data formatting | bytes 65536
  32.6 0.8 %copy.15 = bf16[1,16,64,256]{3,2,1,0:T(8,128)(2,1)} copy(bf16[1,16,64,256]{3,2,1,0:T(8,128)(2,1)S(1)} %get-tuple-element.5) | data formatting | bytes 1048576
Async XLA Ops:
  0.6 0.8 %copy-start.6 = (s32[4]{0:T(128)S(1)}, s32[4]{0:T(128)}, u32[]{:S(2)}) copy-start(s32[4]{0:T(128)} %owner.1) | copy-start | bytes 52
  0.6 0.8 %copy-start.5 = (bf16[1,16]{1,0:T(2,128)(2,1)S(1)}, bf16[1,16]{1,0:T(2,128)(2,1)}, u32[]{:S(2)}) copy-start(bf16[1,16]{1,0:T(2,128)(2,1)} %weight.1) | copy-start | bytes 100
  1.4 1.2 %copy-start = (s32[1,16,64,256]{3,2,1,0:T(8,128)S(1)}, s32[1,16,64,256]{3,2,1,0:T(8,128)}, u32[]{:S(2)}) copy-start(s32[1,16,64,256]{3,2,1,0:T(8,128)} %masks.1) | copy-start | bytes 3145732
  2.6 1.0 %copy-start.1 = (bf16[1,16,64,256]{3,2,1,0:T(8,128)(2,1)S(1)}, bf16[1,16,64,256]{3,2,1,0:T(8,128)(2,1)}, u32[]{:S(2)}) copy-start(bf16[1,16,64,256]{3,2,1,0:T(8,128)(2,1)} %images.1) | copy-start | bytes 1572868
  3.7 1.0 %copy-start.2 = (bf16[3,256,256]{2,1,0:T(8,128)(2,1)S(1)}, bf16[3,256,256]{2,1,0:T(8,128)(2,1)}, u32[]{:S(2)}) copy-start(bf16[3,256,256]{2,1,0:T(8,128)(2,1)} %constant.6.clone.across_in) | copy-start | bytes 1179652
  4.7 0.9 %copy-start.3 = (f32[48,432]{1,0:T(8,128)S(1)}, f32[48,432]{1,0:T(8,128)}, u32[]{:S(2)}) copy-start(f32[48,432]{1,0:T(8,128)} %constant.8.clone.collect_in) | copy-start | bytes 248836
  5.6 0.8 %copy-start.4 = (bf16[192,96]{1,0:T(8,128)(2,1)S(1)}, bf16[192,96]{1,0:T(8,128)(2,1)}, u32[]{:S(2)}) copy-start(bf16[192,96]{1,0:T(8,128)(2,1)} %constant.7.clone.vertical_in) | copy-start | bytes 110596
where the time goes:
time: 33.7 us; the launch traced here: 33.4 us
  Pallas kernels  25.6 us (76%)
  local copies, waits for them, and re-layouts  7.11 us (21%)
  between operations  0.66 us (2%)
    pallas_call x1, Pallas kernels, body(): pl.pallas_call(functools.partial(kernel, visits, strips, distinct), out_s...  25.6 us
    unnamed x17, local copies, waits for them, and re-layouts  7.11 us

commit v1 on v0

--- a/solution.py
+++ b/solution.py
@@ -63,22 +63,23 @@
 def kernel(
     visits, strips, distinct,
     images, masks, weight, cross, owner, cross_scalar, across_in, vertical_in, collect_in,
-    coadd_out, diff_out,
-    image_v, mask_v, across, vertical, collect, use, use_image, sums, send, recv, gath,
-    basis, prods, small, small_in, diff_v,
-    in_sem, const_sem, out_sem, rs_send, rs_recv, ag_send, ag_recv, halo_send, halo_recv,
+    coadd_out, image_v, basis, mixers,
+    mask_v, across, vertical, collect, use, use_image, sums, send, recv, gath,
+    prods, small, small_in,
+    in_sem, const_sem, rs_send, rs_recv, ag_send, ag_recv, halo_send, halo_recv,
     st_send, st_recv,
 ):
     pieces, rows, cols = images.shape[1:]
     blocks = rows // TILE
     span = pieces * TILE
+    order = [0] + ([blocks - 1] if blocks > 1 else []) + list(range(1, blocks - 1))
     me = lax.axis_index("visit")
     strip = lax.axis_index("strip")
 
-    loads = []
-    for t in range(blocks):
+    loads = {}
+    for t in order:
         piece_rows = pl.ds(t * TILE, TILE)
-        loads.append((
+        loads[t] = ((
             pltpu.make_async_copy(masks.at[0, :, piece_rows, :], mask_v.at[t], in_sem.at[0, t]),
             pltpu.make_async_copy(images.at[0, :, piece_rows, :], image_v.at[t], in_sem.at[1, t]),
         ))
@@ -87,8 +88,8 @@
         pltpu.make_async_copy(vertical_in, vertical, const_sem.at[1]),
         pltpu.make_async_copy(collect_in, collect, const_sem.at[2]),
     ]
-    for pair in loads:
-        for copy in pair:
+    for t in order:
+        for copy in loads[t]:
             copy.start()
     for copy in constants:
         copy.start()
@@ -107,12 +108,12 @@
             target = {"visit": other_visit(k), "strip": lax.rem(strip + hop, strips)}
             pl.semaphore_signal(barrier, inc=1, device_id=target, device_id_type=MESH)
 
-    position = jnp.zeros((pieces, 1), jnp.int32)
+    position = jnp.zeros((1, pieces), jnp.int32)
     for p in range(visits):
         position = position + jnp.where(cross[...] == p, owner[p], 0)
-    one_hot = (position == iota((pieces, 128), 1)).astype(F32).astype(BF16)
+    one_hot = (position == iota((128, pieces), 0)).astype(F32).astype(BF16)
     eq = (jnp.right_shift(iota((visits * TILE, 128), 0), 4) == iota((visits * TILE, 128), 1))
-    spread = nt(eq.astype(F32).astype(BF16), one_hot)
+    spread = nn(eq.astype(F32).astype(BF16), one_hot)
     spread = (spread * weight[...].astype(F32)).astype(BF16)
     e2 = iota((pieces, span), 0) == jnp.right_shift(iota((pieces, span), 1), 4)
     wide = nn(spread, e2.astype(F32).astype(BF16))
@@ -122,9 +123,9 @@
     adder = jnp.where(same, wide, 0.0).astype(BF16)
     e_rows = jnp.right_shift(iota((span, 128), 0), 4) == iota((span, 128), 1)
     e_rows = e_rows.astype(F32).astype(BF16)
-    row_hot = nn(e_rows[:, :pieces], one_hot)
-
-    seats = [owner[cross_scalar[j, 0]] for j in range(pieces)]
+    row_hot = nt(e_rows[:, :pieces], one_hot)
+
+    seats = [owner[cross_scalar[0, j]] for j in range(pieces)]
     slots = [jnp.int32(0)] * distinct
     rank = jnp.int32(0)
     for q in range(visits):
@@ -135,7 +136,7 @@
             slots[d] = slots[d] + jnp.where((present == 1) & (rank == d), q, 0)
         rank = rank + present
 
-    for t in range(blocks):
+    for t in order:
         for copy in loads[t]:
             copy.wait()
         usable = ((mask_v[t].reshape(span, cols) & 3) != 3).astype(F32).astype(BF16)
@@ -147,20 +148,20 @@
             total = nn(adder, value)
             for q in range(visits):
                 block = total[q * TILE : (q + 1) * TILE]
-                sums[q, part, pl.ds(t * TILE, TILE), :] = block
-                send[q, part, pl.ds(t * TILE, TILE), :] = block.astype(BF16)
+                sums[t, q, part] = block
+                send[t, q, part] = block.astype(BF16)
 
     pl.semaphore_wait(barrier, visits * strips - 1)
 
-    copies = []
-    for k in range(1, visits):
-        copies.append(pltpu.make_async_remote_copy(
-            src_ref=send.at[other_visit(k)], dst_ref=recv.at[k - 1],
-            send_sem=rs_send.at[k - 1], recv_sem=rs_recv.at[k - 1],
-            device_id={"visit": other_visit(k)}, device_id_type=MESH,
-        ))
-    for copy in copies:
-        copy.start()
+    reduces = {}
+    for t in order:
+        for k in range(visits - 1, 0, -1):
+            reduces[t, k] = pltpu.make_async_remote_copy(
+                src_ref=send.at[t, other_visit(k)], dst_ref=recv.at[t, k - 1],
+                send_sem=rs_send.at[t, k - 1], recv_sem=rs_recv.at[t, k - 1],
+                device_id={"visit": other_visit(k)}, device_id_type=MESH,
+            )
+            reduces[t, k].start()
 
     @pl.when(jnp.logical_not(above))
     def _():
@@ -170,23 +171,6 @@
     def _():
         gath[:, pl.ds(TILE + rows, TILE), :] = jnp.zeros((visits, TILE, cols), BF16)
 
-    numerator = sums[me, 0]
-    denominator = sums[me, 1]
-    for k in range(1, visits):
-        copies[k - 1].wait_recv()
-        numerator = numerator + recv[k - 1, 0].astype(F32)
-        denominator = denominator + recv[k - 1, 1].astype(F32)
-    coadd = (numerator / jnp.maximum(denominator, 1.0)).astype(BF16)
-    gath[me, pl.ds(TILE, rows), :] = coadd
-
-    mains = []
-    for k in range(1, visits):
-        place = gath.at[me, pl.ds(TILE, rows)]
-        mains.append(pltpu.make_async_remote_copy(
-            src_ref=place, dst_ref=place,
-            send_sem=ag_send.at[k - 1], recv_sem=ag_recv.at[k - 1],
-            device_id={"visit": other_visit(k)}, device_id_type=MESH,
-        ))
     downs, ups = [], []
     for k in range(visits):
         downs.append(pltpu.make_async_remote_copy(
@@ -201,27 +185,40 @@
             device_id={"visit": other_visit(k), "strip": lax.rem(strip + strips - 1, strips)},
             device_id_type=MESH,
         ))
-    for copy in mains:
-        copy.start()
-
-    @pl.when(below)
-    def _():
-        for copy in downs:
-            copy.start()
-
-    @pl.when(above)
-    def _():
-        for copy in ups:
-            copy.start()
-
-    coadd_copy = pltpu.make_async_copy(
-        gath.at[me, pl.ds(TILE, rows)], coadd_out.at[0, 0], out_sem.at[0]
-    )
-    coadd_copy.start()
+    gathers = {}
+    for t in order:
+        numerator = sums[t, me, 0]
+        denominator = sums[t, me, 1]
+        for k in range(1, visits):
+            reduces[t, k].wait_recv()
+            numerator = numerator + recv[t, k - 1, 0].astype(F32)
+            denominator = denominator + recv[t, k - 1, 1].astype(F32)
+        coadd = (numerator / jnp.maximum(denominator, 1.0)).astype(BF16)
+        gath[me, pl.ds(TILE + t * TILE, TILE), :] = coadd
+        coadd_out[pl.ds(t * TILE, TILE), :] = coadd
+        for k in range(1, visits):
+            place = gath.at[me, pl.ds(TILE + t * TILE, TILE)]
+            gathers[t, k] = pltpu.make_async_remote_copy(
+                src_ref=place, dst_ref=place,
+                send_sem=ag_send.at[t, k - 1], recv_sem=ag_recv.at[t, k - 1],
+                device_id={"visit": other_visit(k)}, device_id_type=MESH,
+            )
+            gathers[t, k].start()
+
+        if t == blocks - 1:
+            @pl.when(below)
+            def _():
+                for copy in downs:
+                    copy.start()
+
+        if t == 0:
+            @pl.when(above)
+            def _():
+                for copy in ups:
+                    copy.start()
+
     for copy in constants:
         copy.wait()
-    for copy in mains:
-        copy.wait_recv()
 
     @pl.when(above)
     def _():
@@ -232,6 +229,10 @@
     def _():
         for copy in ups:
             copy.wait_recv()
+
+    for t in order:
+        for k in range(1, visits):
+            gathers[t, k].wait_recv()
 
     for d in range(distinct):
         template = gath[slots[d]]
@@ -317,8 +318,29 @@
     )
     e3 = (source == iota((16, wide_c), 0)).astype(F32).astype(BF16)
     mixer = jnp.where(keep(wide_c), nn(by_row, e3), 0.0)
-    mixers = [(mixer * member(d)).astype(BF16) for d in range(distinct)]
-    stores = []
+    for d in range(distinct):
+        mixers[d] = (mixer * member(d)).astype(BF16)
+
+    for copy in list(reduces.values()) + list(gathers.values()) + exchanges:
+        copy.wait_send()
+
+    @pl.when(below)
+    def _():
+        for copy in downs:
+            copy.wait_send()
+
+    @pl.when(above)
+    def _():
+        for copy in ups:
+            copy.wait_send()
+
+
+def finish(coadd_in, image_v, basis, mixers, coadd_out, diff_out, diff_v, out_sem):
+    distinct = basis.shape[0]
+    blocks, pieces, _, cols = image_v.shape
+    span = pieces * TILE
+    stores = [pltpu.make_async_copy(coadd_in, coadd_out.at[0, 0], out_sem.at[0])]
+    stores[0].start()
     for t in range(blocks):
         lanes = pl.ds(t * cols, cols)
         fitted = jnp.zeros((span, cols), F32)
@@ -332,21 +354,6 @@
         )
         copy.start()
         stores.append(copy)
-
-    for copy in copies + mains + exchanges:
-        copy.wait_send()
-
-    @pl.when(below)
-    def _():
-        for copy in downs:
-            copy.wait_send()
-
-    @pl.when(above)
-    def _():
-        for copy in ups:
-            copy.wait_send()
-
-    coadd_copy.wait()
     for copy in stores:
         copy.wait()
 
@@ -363,56 +370,67 @@
         BF16,
     )
     collect = jnp.asarray(gather_matrix())
-    anywhere = pl.BlockSpec(memory_space=pl.ANY)
+    hbm = pl.BlockSpec(memory_space=pltpu.HBM)
     vmem = pl.BlockSpec(memory_space=pltpu.VMEM)
     smem = pl.BlockSpec(memory_space=pltpu.SMEM)
     dma = pltpu.SemaphoreType.DMA
     peers = max(1, visits - 1)
-    return pl.pallas_call(
+    cross = intersection.reshape(1, pieces)
+    middle = pl.pallas_call(
         functools.partial(kernel, visits, strips, distinct),
         out_shape=(
-            jax.ShapeDtypeStruct((1, 1, rows, cols), BF16),
-            jax.ShapeDtypeStruct(images.shape, BF16),
+            jax.ShapeDtypeStruct((rows, cols), BF16),
+            jax.ShapeDtypeStruct((blocks, pieces, TILE, cols), BF16),
+            jax.ShapeDtypeStruct((distinct, BASES * TILE, blocks * cols), BF16),
+            jax.ShapeDtypeStruct((distinct, span, 2 * BASES * TILE), BF16),
         ),
-        in_specs=[anywhere, anywhere, vmem, vmem, smem, smem, anywhere, anywhere, anywhere],
-        out_specs=(anywhere, anywhere),
+        in_specs=[hbm, hbm, vmem, vmem, smem, smem, hbm, hbm, hbm],
+        out_specs=(vmem, vmem, vmem, vmem),
         scratch_shapes=[
-            pltpu.VMEM((blocks, pieces, TILE, cols), BF16),
             pltpu.VMEM((blocks, pieces, TILE, cols), jnp.int32),
             pltpu.VMEM(across.shape, BF16),
             pltpu.VMEM(vertical.shape, BF16),
             pltpu.VMEM(collect.shape, F32),
             pltpu.VMEM((span, blocks * cols), BF16),
             pltpu.VMEM((span, blocks * cols), BF16),
-            pltpu.VMEM((visits, 2, rows, cols), F32),
-            pltpu.VMEM((visits, 2, rows, cols), BF16),
-            pltpu.VMEM((peers, 2, rows, cols), BF16),
+            pltpu.VMEM((blocks, visits, 2, TILE, cols), F32),
+            pltpu.VMEM((blocks, visits, 2, TILE, cols), BF16),
+            pltpu.VMEM((blocks, peers, 2, TILE, cols), BF16),
             pltpu.VMEM((visits, rows + 2 * TILE, cols), BF16),
-            pltpu.VMEM((distinct, BASES * TILE, blocks * cols), BF16),
             pltpu.VMEM((distinct, len(pairs) * TILE, blocks * cols), BF16),
             pltpu.VMEM((BASES * 8, 128), F32),
             pltpu.VMEM((max(1, strips - 1), BASES * 8, 128), F32),
-            pltpu.VMEM((blocks, pieces, TILE, cols), BF16),
             dma((2, blocks)),
             dma((3,)),
-            dma((1 + blocks,)),
-            dma((peers,)),
-            dma((peers,)),
-            dma((peers,)),
-            dma((peers,)),
+            dma((blocks, peers)),
+            dma((blocks, peers)),
+            dma((blocks, peers)),
+            dma((blocks, peers)),
             dma((2, visits)),
             dma((2, visits)),
             dma((max(1, strips - 1),)),
             dma((max(1, strips - 1),)),
         ],
         compiler_params=pltpu.CompilerParams(
-            collective_id=0, has_side_effects=True, vmem_limit_bytes=48 * 1024 * 1024
+            collective_id=0, has_side_effects=True, vmem_limit_bytes=40 * 1024 * 1024
         ),
-        name="coadd_difference",
+        name="coadd_solve",
     )(
-        images, mask_bits, visit_weight, intersection, patch_owner, intersection,
+        images, mask_bits, visit_weight, cross, patch_owner, cross,
         across, vertical, collect,
     )
+    return pl.pallas_call(
+        finish,
+        out_shape=(
+            jax.ShapeDtypeStruct((1, 1, rows, cols), BF16),
+            jax.ShapeDtypeStruct(images.shape, BF16),
+        ),
+        in_specs=[vmem, vmem, vmem, vmem],
+        out_specs=(hbm, hbm),
+        scratch_shapes=[pltpu.VMEM((blocks, pieces, TILE, cols), BF16), dma((1 + blocks,))],
+        compiler_params=pltpu.CompilerParams(vmem_limit_bytes=32 * 1024 * 1024),
+        name="difference",
+    )(*middle)
 
 
 def solution(mesh):

time: 33.7 us -> 32.4 us (0.961)
  local copies, waits for them, and re-layouts: 7.11 us -> 5.61 us
    unnamed x17 -> x16, local copies, waits for them, and re-layouts: 7.11 us -> 5.61 us
    pallas_call x0 -> x1, Pallas kernels: none -> 1.18 us  [body(): pl.pallas_call(finish, out_shape=(jax.ShapeDtypeStruct((1, 1, rows, cols)...]
    pallas_call x1, Pallas kernels: 25.6 us -> 24.6 us  [body(): pl.pallas_call(functools.partial(kernel, visits, strips, distinct), out_s...]
where the time goes in v1:
time: 32.4 us; the launch traced here: 32.1 us
  Pallas kernels  25.8 us (80%)
  local copies, waits for them, and re-layouts  5.61 us (17%)
  between operations  0.67 us (2%)
    pallas_call x1, Pallas kernels, body(): pl.pallas_call(functools.partial(kernel, visits, strips, distinct), out_s...  24.6 us
    unnamed x16, local copies, waits for them, and re-layouts  5.61 us
    pallas_call x1, Pallas kernels, body(): pl.pallas_call(finish, out_shape=(jax.ShapeDtypeStruct((1, 1, rows, cols)...  1.18 us

profile of v1, /device:TPU:0, one launch (start us, length us, event | category | flops | bytes accessed | tf_op | source)
XLA Modules:
  0.0 32.1 jit_solution(10006354085905441859)
XLA Ops:
  0.6 0.0 copy-start.7
  0.6 0.0 copy-start.5
  0.7 0.0 copy-start.6
  0.7 0.6 %copy-done.7 = s32[4]{0:T(128)S(1)} copy-done((s32[4]{0:T(128)S(1)}, s32[4]{0:T(128)}, u32[]{:S(2)}) %copy-start.7) | copy-done | bytes 40
  1.3 0.0 copy-done.5
  1.3 0.0 copy-done.6
  1.3 0.0 copy-start
  1.3 1.2 %copy-done = s32[1,16,64,256]{3,2,1,0:T(8,128)S(1)} copy-done((s32[1,16,64,256]{3,2,1,0:T(8,128)S(1)}, s32[1,16,64,256]{3,2,1,0:T(8,128)}, u32[]{:S(2)}) %copy-start) | copy-done | bytes 1048600
  2.5 0.0 copy-start.1
  2.5 1.0 %copy-done.1 = bf16[1,16,64,256]{3,2,1,0:T(8,128)(2,1)S(1)} copy-done((bf16[1,16,64,256]{3,2,1,0:T(8,128)(2,1)S(1)}, bf16[1,16,64,256]{3,2,1,0:T(8,128)(2,1)}, u32[]{:S(2)}) %copy-start.1) | copy-done | bytes 524312
  3.6 0.0 copy-start.2
  3.6 1.0 %copy-done.2 = bf16[3,256,256]{2,1,0:T(8,128)(2,1)S(1)} copy-done((bf16[3,256,256]{2,1,0:T(8,128)(2,1)S(1)}, bf16[3,256,256]{2,1,0:T(8,128)(2,1)}, u32[]{:S(2)}) %copy-start.2) | copy-done | bytes 393240
  4.6 0.0 copy-start.3
  4.6 0.9 %copy-done.3 = f32[48,432]{1,0:T(8,128)S(1)} copy-done((f32[48,432]{1,0:T(8,128)S(1)}, f32[48,432]{1,0:T(8,128)}, u32[]{:S(2)}) %copy-start.3) | copy-done | bytes 82968
  5.5 0.0 copy-start.4
  5.5 0.8 %copy-done.4 = bf16[192,96]{1,0:T(8,128)(2,1)S(1)} copy-done((bf16[192,96]{1,0:T(8,128)(2,1)S(1)}, bf16[192,96]{1,0:T(8,128)(2,1)}, u32[]{:S(2)}) %copy-start.4) | copy-done | bytes 36888
  6.3 24.6 %coadd_solve.1 = (bf16[64,256]{1,0:T(8,128)(2,1)S(1)}, bf16[4,16,16,256]{3,2,1,0:T(8,128)(2,1)S(1)}, bf16[2,96,1024]{2,1,0:T(8,128)(2,1)S(1)}, bf16[2,256,192]{2,1,0:T(8,128)(2,1)S(1)}) custom-call(bf16[1,16,64,256]{3,2,1,0:T(8,128)(2,1)S(1)} %copy-done.1, s32[1,16,64,256]{3,2,1,0:T(8,128)S(1)} %copy-done, bf16[1,16]{1,0:T(2,128)(2,1)S(1)} %copy-done.6, ...), custom_call_target="tpu_custom_call" | custom-call | tf_op jit(solution)/shard_map/coadd_solve/pallas_call | solution.py:379
  30.9 1.2 %difference.1 = (bf16[1,1,64,256]{3,2,1,0:T(8,128)(2,1)}, bf16[1,16,64,256]{3,2,1,0:T(8,128)(2,1)}) custom-call(bf16[64,256]{1,0:T(8,128)(2,1)S(1)} %get-tuple-element.6.coadd_in, bf16[4,16,16,256]{3,2,1,0:T(8,128)(2,1)S(1)} %get-tuple-element.7.image_v, bf16[2,96,1024]{2,1,0:T(8,128)(2,1)S(1)} %get-tuple-element.8.basis, ...), custom_call_target="tpu_custom_call" | custom-call | tf_op jit(solution)/shard_map/difference/pallas_call | solution.py:422
Async XLA Ops:
  0.6 0.7 %copy-start.7 = (s32[4]{0:T(128)S(1)}, s32[4]{0:T(128)}, u32[]{:S(2)}) copy-start(s32[4]{0:T(128)} %owner.1) | copy-start | bytes 52
  0.6 0.7 %copy-start.5 = (s32[16,1]{0,1:T(1,128)S(1)}, s32[16,1]{0,1:T(1,128)}, u32[]{:S(2)}) copy-start(s32[16,1]{0,1:T(1,128)} %param.11) | copy-start | bytes 196
  0.7 0.7 %copy-start.6 = (bf16[1,16]{1,0:T(2,128)(2,1)S(1)}, bf16[1,16]{1,0:T(2,128)(2,1)}, u32[]{:S(2)}) copy-start(bf16[1,16]{1,0:T(2,128)(2,1)} %weight.1) | copy-start | bytes 100
  1.3 1.2 %copy-start = (s32[1,16,64,256]{3,2,1,0:T(8,128)S(1)}, s32[1,16,64,256]{3,2,1,0:T(8,128)}, u32[]{:S(2)}) copy-start(s32[1,16,64,256]{3,2,1,0:T(8,128)} %masks.1) | copy-start | bytes 3145732
  2.5 1.0 %copy-start.1 = (bf16[1,16,64,256]{3,2,1,0:T(8,128)(2,1)S(1)}, bf16[1,16,64,256]{3,2,1,0:T(8,128)(2,1)}, u32[]{:S(2)}) copy-start(bf16[1,16,64,256]{3,2,1,0:T(8,128)(2,1)} %images.1) | copy-start | bytes 1572868
  3.6 1.0 %copy-start.2 = (bf16[3,256,256]{2,1,0:T(8,128)(2,1)S(1)}, bf16[3,256,256]{2,1,0:T(8,128)(2,1)}, u32[]{:S(2)}) copy-start(bf16[3,256,256]{2,1,0:T(8,128)(2,1)} %constant.6.clone.across_in) | copy-start | bytes 1179652
  4.6 0.9 %copy-start.3 = (f32[48,432]{1,0:T(8,128)S(1)}, f32[48,432]{1,0:T(8,128)}, u32[]{:S(2)}) copy-start(f32[48,432]{1,0:T(8,128)} %constant.8.clone.collect_in) | copy-start | bytes 248836
  5.5 0.8 %copy-start.4 = (bf16[192,96]{1,0:T(8,128)(2,1)S(1)}, bf16[192,96]{1,0:T(8,128)(2,1)}, u32[]{:S(2)}) copy-start(bf16[192,96]{1,0:T(8,128)(2,1)} %constant.7.clone.vertical_in) | copy-start | bytes 110596

commit v2 on v1

--- a/solution.py
+++ b/solution.py
@@ -62,9 +62,9 @@
 
 def kernel(
     visits, strips, distinct,
-    images, masks, weight, cross, owner, cross_scalar, across_in, vertical_in, collect_in,
+    images, masks, weight, cross, owner, cross_scalar, table_in,
     coadd_out, image_v, basis, mixers,
-    mask_v, across, vertical, collect, use, use_image, sums, send, recv, gath,
+    mask_v, tables, use, use_image, sums, send, recv, gath,
     prods, small, small_in,
     in_sem, const_sem, rs_send, rs_recv, ag_send, ag_recv, halo_send, halo_recv,
     st_send, st_recv,
@@ -83,11 +83,7 @@
             pltpu.make_async_copy(masks.at[0, :, piece_rows, :], mask_v.at[t], in_sem.at[0, t]),
             pltpu.make_async_copy(images.at[0, :, piece_rows, :], image_v.at[t], in_sem.at[1, t]),
         ))
-    constants = [
-        pltpu.make_async_copy(across_in, across, const_sem.at[0]),
-        pltpu.make_async_copy(vertical_in, vertical, const_sem.at[1]),
-        pltpu.make_async_copy(collect_in, collect, const_sem.at[2]),
-    ]
+    constants = [pltpu.make_async_copy(table_in, tables, const_sem)]
     for t in order:
         for copy in loads[t]:
             copy.start()
@@ -234,13 +230,20 @@
         for k in range(1, visits):
             gathers[t, k].wait_recv()
 
+    top = BASES // 2 * cols
+    vertical = tables[pl.ds(top, 3 * rows), pl.ds(0, rows + 2 * TILE)]
+    top = top + 3 * rows
+
+    def across(c):
+        return tables[pl.ds(c * cols, cols), pl.ds(0, cols)]
+
     for d in range(distinct):
         template = gath[slots[d]]
-        smooth = nn(vertical[...], template).astype(BF16)
+        smooth = nn(vertical, template).astype(BF16)
         planes = [None] * BASES
         for c in range(3):
             taken = [a for a in range(BASES) if basis_cols[a] == c]
-            product = nn(smooth[: len(taken) * rows], across[c]).astype(BF16)
+            product = nn(smooth[: len(taken) * rows], across(c)).astype(BF16)
             for a in taken:
                 r = basis_rows[a]
                 planes[a] = product[r * rows : (r + 1) * rows]
@@ -274,8 +277,10 @@
         mine = member(d)
         normal = normal + summed(jnp.where(keep(wide_n), nt(use[...], prods[d]), 0.0) * mine)
         right = right + summed(jnp.where(keep(wide_b), nt(use_image[...], basis[d]), 0.0) * mine)
-    system = nt(collect[:, :wide_n], normal, lax.Precision.HIGHEST) + nt(
-        collect[:, wide_n:], right, lax.Precision.HIGHEST
+    normal_rows = tables[pl.ds(top, BASES * 8), pl.ds(0, wide_n)].astype(F32)
+    right_rows = tables[pl.ds(top, BASES * 8), pl.ds(wide_n, wide_b)].astype(F32)
+    system = nt(normal_rows, normal, lax.Precision.HIGHEST) + nt(
+        right_rows, right, lax.Precision.HIGHEST
     )
     small[...] = jnp.concatenate(
         [system, jnp.zeros((BASES * 8, 128 - pieces), F32)], axis=1
@@ -364,12 +369,17 @@
     distinct = max(1, patch_owner.shape[0] // 2)
     span = pieces * TILE
     taps = kernel_taps()
-    across = jnp.asarray(np.transpose(band_matrix(taps, cols, cols, HALF), (0, 2, 1)), BF16)
-    vertical = jnp.asarray(
-        band_matrix(taps, rows, rows + 2 * TILE, HALF - TILE).reshape(3 * rows, rows + 2 * TILE),
-        BF16,
-    )
-    collect = jnp.asarray(gather_matrix())
+    collect = gather_matrix()
+    width = max(collect.shape[1], cols, rows + 2 * TILE)
+    width = -(-width // 128) * 128
+    tables = jnp.asarray(np.concatenate([
+        np.pad(part, ((0, 0), (0, width - part.shape[1])))
+        for part in (
+            np.transpose(band_matrix(taps, cols, cols, HALF), (0, 2, 1)).reshape(3 * cols, cols),
+            band_matrix(taps, rows, rows + 2 * TILE, HALF - TILE).reshape(3 * rows, -1),
+            collect,
+        )
+    ]), BF16)
     hbm = pl.BlockSpec(memory_space=pltpu.HBM)
     vmem = pl.BlockSpec(memory_space=pltpu.VMEM)
     smem = pl.BlockSpec(memory_space=pltpu.SMEM)
@@ -384,13 +394,11 @@
             jax.ShapeDtypeStruct((distinct, BASES * TILE, blocks * cols), BF16),
             jax.ShapeDtypeStruct((distinct, span, 2 * BASES * TILE), BF16),
         ),
-        in_specs=[hbm, hbm, vmem, vmem, smem, smem, hbm, hbm, hbm],
+        in_specs=[hbm, hbm, vmem, vmem, smem, smem, hbm],
         out_specs=(vmem, vmem, vmem, vmem),
         scratch_shapes=[
             pltpu.VMEM((blocks, pieces, TILE, cols), jnp.int32),
-            pltpu.VMEM(across.shape, BF16),
-            pltpu.VMEM(vertical.shape, BF16),
-            pltpu.VMEM(collect.shape, F32),
+            pltpu.VMEM(tables.shape, BF16),
             pltpu.VMEM((span, blocks * cols), BF16),
             pltpu.VMEM((span, blocks * cols), BF16),
             pltpu.VMEM((blocks, visits, 2, TILE, cols), F32),
@@ -401,7 +409,7 @@
             pltpu.VMEM((BASES * 8, 128), F32),
             pltpu.VMEM((max(1, strips - 1), BASES * 8, 128), F32),
             dma((2, blocks)),
-            dma((3,)),
+            dma,
             dma((blocks, peers)),
             dma((blocks, peers)),
             dma((blocks, peers)),
@@ -412,12 +420,12 @@
             dma((max(1, strips - 1),)),
         ],
         compiler_params=pltpu.CompilerParams(
-            collective_id=0, has_side_effects=True, vmem_limit_bytes=40 * 1024 * 1024
+            collective_id=0, has_side_effects=True, vmem_limit_bytes=55_100_000
         ),
         name="coadd_solve",
     )(
         images, mask_bits, visit_weight, cross, patch_owner, cross,
-        across, vertical, collect,
+        tables,
     )
     return pl.pallas_call(
         finish,
@@ -427,8 +435,11 @@
         ),
         in_specs=[vmem, vmem, vmem, vmem],
         out_specs=(hbm, hbm),
-        scratch_shapes=[pltpu.VMEM((blocks, pieces, TILE, cols), BF16), dma((1 + blocks,))],
-        compiler_params=pltpu.CompilerParams(vmem_limit_bytes=32 * 1024 * 1024),
+        scratch_shapes=[
+            pltpu.VMEM((blocks, pieces, TILE, cols), BF16),
+            dma((1 + blocks,)),
+        ],
+        compiler_params=pltpu.CompilerParams(vmem_limit_bytes=40 * 1024 * 1024),
         name="difference",
     )(*middle)
 

time: 32.4 us -> 26.7 us (0.82)
  local copies, waits for them, and re-layouts: 5.61 us -> 0.66 us
  Pallas kernels: 25.8 us -> 25.3 us
    unnamed x16 -> x6, local copies, waits for them, and re-layouts: 5.61 us -> 0.66 us
    pallas_call x1, Pallas kernels: 24.6 us -> 24.1 us  [body(): pl.pallas_call(functools.partial(kernel, visits, strips, distinct), out_s...]
where the time goes in v2:
time: 26.7 us; the launch traced here: 26.6 us
  Pallas kernels  25.3 us (95%)
  local copies, waits for them, and re-layouts  0.66 us (2%)
  between operations  0.66 us (2%)
    pallas_call x1, Pallas kernels, body(): pl.pallas_call(functools.partial(kernel, visits, strips, distinct), out_s...  24.1 us
    pallas_call x1, Pallas kernels, body(): pl.pallas_call(finish, out_shape=(jax.ShapeDtypeStruct((1, 1, rows, cols)...  1.18 us
    unnamed x6, local copies, waits for them, and re-layouts  0.66 us

profile of v2, /device:TPU:0, one launch (start us, length us, event | category | flops | bytes accessed | tf_op | source)
XLA Modules:
  0.0 26.6 jit_solution(16305569347419742625)
XLA Ops:
  0.6 0.0 copy-start.2
  0.6 0.0 copy-start
  0.7 0.0 copy-start.1
  0.7 0.6 %copy-done.2 = s32[4]{0:T(128)S(1)} copy-done((s32[4]{0:T(128)S(1)}, s32[4]{0:T(128)}, u32[]{:S(2)}) %copy-start.2) | copy-done | bytes 40
  1.3 0.0 copy-done
  1.3 0.0 copy-done.1
  1.3 24.1 %coadd_solve.1 = (bf16[64,256]{1,0:T(8,128)(2,1)S(1)}, bf16[4,16,16,256]{3,2,1,0:T(8,128)(2,1)S(1)}, bf16[2,96,1024]{2,1,0:T(8,128)(2,1)S(1)}, bf16[2,256,192]{2,1,0:T(8,128)(2,1)S(1)}) custom-call(bf16[1,16,64,256]{3,2,1,0:T(8,128)(2,1)} %images.1, s32[1,16,64,256]{3,2,1,0:T(8,128)} %masks.1, bf16[1,16]{1,0:T(2,128)(2,1)S(1)} %copy-done.1, ...), custom_call_target="tpu_custom_call" | custom-call | tf_op jit(solution)/shard_map/coadd_solve/pallas_call | solution.py:389
  25.4 1.2 %difference.1 = (bf16[1,1,64,256]{3,2,1,0:T(8,128)(2,1)}, bf16[1,16,64,256]{3,2,1,0:T(8,128)(2,1)}) custom-call(bf16[64,256]{1,0:T(8,128)(2,1)S(1)} %get-tuple-element.6.coadd_in, bf16[4,16,16,256]{3,2,1,0:T(8,128)(2,1)S(1)} %get-tuple-element.7.image_v, bf16[2,96,1024]{2,1,0:T(8,128)(2,1)S(1)} %get-tuple-element.8.basis, ...), custom_call_target="tpu_custom_call" | custom-call | tf_op jit(solution)/shard_map/difference/pallas_call | solution.py:430
Async XLA Ops:
  0.6 0.7 %copy-start.2 = (s32[4]{0:T(128)S(1)}, s32[4]{0:T(128)}, u32[]{:S(2)}) copy-start(s32[4]{0:T(128)} %owner.1) | copy-start | bytes 52
  0.6 0.7 %copy-start = (s32[16,1]{0,1:T(1,128)S(1)}, s32[16,1]{0,1:T(1,128)}, u32[]{:S(2)}) copy-start(s32[16,1]{0,1:T(1,128)} %param.9) | copy-start | bytes 196
  0.7 0.7 %copy-start.1 = (bf16[1,16]{1,0:T(2,128)(2,1)S(1)}, bf16[1,16]{1,0:T(2,128)(2,1)}, u32[]{:S(2)}) copy-start(bf16[1,16]{1,0:T(2,128)(2,1)} %weight.1) | copy-start | bytes 100

commit v3 on v2

--- a/solution.py
+++ b/solution.py
@@ -64,9 +64,10 @@
     visits, strips, distinct,
     images, masks, weight, cross, owner, cross_scalar, table_in,
     coadd_out, image_v, basis, mixers,
-    mask_v, tables, use, use_image, sums, send, recv, gath,
+    mask_v, tables, use, use_image, send, recv, ids_own, ids, gath,
     prods, small, small_in,
-    in_sem, const_sem, rs_send, rs_recv, ag_send, ag_recv, halo_send, halo_recv,
+    in_sem, const_sem, rs_send, rs_recv, id_send, id_recv, ag_send, ag_recv,
+    halo_send, halo_recv,
     st_send, st_recv,
 ):
     pieces, rows, cols = images.shape[1:]
@@ -104,23 +105,6 @@
             target = {"visit": other_visit(k), "strip": lax.rem(strip + hop, strips)}
             pl.semaphore_signal(barrier, inc=1, device_id=target, device_id_type=MESH)
 
-    position = jnp.zeros((1, pieces), jnp.int32)
-    for p in range(visits):
-        position = position + jnp.where(cross[...] == p, owner[p], 0)
-    one_hot = (position == iota((128, pieces), 0)).astype(F32).astype(BF16)
-    eq = (jnp.right_shift(iota((visits * TILE, 128), 0), 4) == iota((visits * TILE, 128), 1))
-    spread = nn(eq.astype(F32).astype(BF16), one_hot)
-    spread = (spread * weight[...].astype(F32)).astype(BF16)
-    e2 = iota((pieces, span), 0) == jnp.right_shift(iota((pieces, span), 1), 4)
-    wide = nn(spread, e2.astype(F32).astype(BF16))
-    same = (iota((visits * TILE, span), 0) & (TILE - 1)) == (
-        iota((visits * TILE, span), 1) & (TILE - 1)
-    )
-    adder = jnp.where(same, wide, 0.0).astype(BF16)
-    e_rows = jnp.right_shift(iota((span, 128), 0), 4) == iota((span, 128), 1)
-    e_rows = e_rows.astype(F32).astype(BF16)
-    row_hot = nt(e_rows[:, :pieces], one_hot)
-
     seats = [owner[cross_scalar[0, j]] for j in range(pieces)]
     slots = [jnp.int32(0)] * distinct
     rank = jnp.int32(0)
@@ -132,6 +116,23 @@
             slots[d] = slots[d] + jnp.where((present == 1) & (rank == d), q, 0)
         rank = rank + present
 
+    position = jnp.zeros((1, pieces), jnp.int32)
+    for p in range(visits):
+        position = position + jnp.where(cross[...] == p, owner[p], 0)
+    one_hot = (position == iota((128, pieces), 0)).astype(F32).astype(BF16)
+    eq = jnp.concatenate([iota((TILE, 128), 1) == slots[d] for d in range(distinct)], axis=0)
+    spread = nn(eq.astype(F32).astype(BF16), one_hot)
+    spread = (spread * weight[...].astype(F32)).astype(BF16)
+    e2 = iota((pieces, span), 0) == jnp.right_shift(iota((pieces, span), 1), 4)
+    wide = nn(spread, e2.astype(F32).astype(BF16))
+    same = (iota((distinct * TILE, span), 0) & (TILE - 1)) == (
+        iota((distinct * TILE, span), 1) & (TILE - 1)
+    )
+    adder = jnp.where(same, wide, 0.0).astype(BF16)
+    e_rows = jnp.right_shift(iota((span, 128), 0), 4) == iota((span, 128), 1)
+    e_rows = e_rows.astype(F32).astype(BF16)
+    row_hot = nt(e_rows[:, :pieces], one_hot)
+
     for t in order:
         for copy in loads[t]:
             copy.wait()
@@ -142,93 +143,119 @@
         use_image[:, lanes] = masked
         for part, value in enumerate((masked, usable)):
             total = nn(adder, value)
-            for q in range(visits):
-                block = total[q * TILE : (q + 1) * TILE]
-                sums[t, q, part] = block
-                send[t, q, part] = block.astype(BF16)
+            for d in range(distinct):
+                send[t, d, part] = total[d * TILE : (d + 1) * TILE].astype(BF16)
+    names = jnp.zeros((1, 128), jnp.int32)
+    for d in range(distinct):
+        names = names + jnp.where(iota((1, 128), 1) == d, slots[d], 0)
+    ids_own[...] = names.astype(F32)
 
     pl.semaphore_wait(barrier, visits * strips - 1)
 
-    reduces = {}
-    for t in order:
-        for k in range(visits - 1, 0, -1):
-            reduces[t, k] = pltpu.make_async_remote_copy(
-                src_ref=send.at[t, other_visit(k)], dst_ref=recv.at[t, k - 1],
-                send_sem=rs_send.at[t, k - 1], recv_sem=rs_recv.at[t, k - 1],
-                device_id={"visit": other_visit(k)}, device_id_type=MESH,
-            )
-            reduces[t, k].start()
+    def block_of(r):
+        return r ^ 1 if blocks % 2 == 0 else r
+
+    my_block = me + 1 - 2 * lax.rem(me, 2) if blocks % 2 == 0 else me
+
+    def reduce_copies(r, source):
+        return (
+            pltpu.make_async_remote_copy(
+                src_ref=ids_own, dst_ref=ids.at[source],
+                send_sem=id_send.at[r], recv_sem=id_recv.at[source],
+                device_id={"visit": r}, device_id_type=MESH,
+            ),
+            pltpu.make_async_remote_copy(
+                src_ref=send.at[block_of(r)], dst_ref=recv.at[source],
+                send_sem=rs_send.at[r], recv_sem=rs_recv.at[source],
+                device_id={"visit": r}, device_id_type=MESH,
+            ),
+        )
+
+    def gather_copy(v, block):
+        return pltpu.make_async_remote_copy(
+            src_ref=gath.at[1 + block], dst_ref=gath.at[1 + block],
+            send_sem=ag_send.at[v], recv_sem=ag_recv.at[block],
+            device_id={"visit": v}, device_id_type=MESH,
+        )
+
+    for r in range(blocks):
+        @pl.when(me != r)
+        def _():
+            for copy in reduce_copies(r, me):
+                copy.start()
 
     @pl.when(jnp.logical_not(above))
     def _():
-        gath[:, pl.ds(0, TILE), :] = jnp.zeros((visits, TILE, cols), BF16)
+        gath[0] = jnp.zeros((visits, TILE, cols), BF16)
 
     @pl.when(jnp.logical_not(below))
     def _():
-        gath[:, pl.ds(TILE + rows, TILE), :] = jnp.zeros((visits, TILE, cols), BF16)
-
-    downs, ups = [], []
-    for k in range(visits):
-        downs.append(pltpu.make_async_remote_copy(
-            src_ref=gath.at[me, pl.ds(rows, TILE)], dst_ref=gath.at[me, pl.ds(0, TILE)],
-            send_sem=halo_send.at[0, k], recv_sem=halo_recv.at[0, k],
-            device_id={"visit": other_visit(k), "strip": lax.rem(strip + 1, strips)},
-            device_id_type=MESH,
-        ))
-        ups.append(pltpu.make_async_remote_copy(
-            src_ref=gath.at[me, pl.ds(TILE, TILE)], dst_ref=gath.at[me, pl.ds(TILE + rows, TILE)],
-            send_sem=halo_send.at[1, k], recv_sem=halo_recv.at[1, k],
-            device_id={"visit": other_visit(k), "strip": lax.rem(strip + strips - 1, strips)},
-            device_id_type=MESH,
-        ))
-    gathers = {}
-    for t in order:
-        numerator = sums[t, me, 0]
-        denominator = sums[t, me, 1]
-        for k in range(1, visits):
-            reduces[t, k].wait_recv()
-            numerator = numerator + recv[t, k - 1, 0].astype(F32)
-            denominator = denominator + recv[t, k - 1, 1].astype(F32)
-        coadd = (numerator / jnp.maximum(denominator, 1.0)).astype(BF16)
-        gath[me, pl.ds(TILE + t * TILE, TILE), :] = coadd
-        coadd_out[pl.ds(t * TILE, TILE), :] = coadd
-        for k in range(1, visits):
-            place = gath.at[me, pl.ds(TILE + t * TILE, TILE)]
-            gathers[t, k] = pltpu.make_async_remote_copy(
-                src_ref=place, dst_ref=place,
-                send_sem=ag_send.at[t, k - 1], recv_sem=ag_recv.at[t, k - 1],
-                device_id={"visit": other_visit(k)}, device_id_type=MESH,
-            )
-            gathers[t, k].start()
-
-        if t == blocks - 1:
-            @pl.when(below)
+        gath[blocks + 1] = jnp.zeros((visits, TILE, cols), BF16)
+
+    def reduce():
+        recv[me] = send[my_block]
+        ids[me] = ids_own[...]
+        for v in range(visits):
+            @pl.when(me != v)
             def _():
-                for copy in downs:
-                    copy.start()
-
-        if t == 0:
-            @pl.when(above)
+                for copy in reduce_copies(0, v):
+                    copy.wait_recv()
+
+        def one_patch(q, carry):
+            numerator = jnp.zeros((TILE, cols), F32)
+            denominator = jnp.zeros((TILE, cols), F32)
+            number = lax.convert_element_type(q, F32)
+            for v in range(visits):
+                for d in range(distinct):
+                    here = jnp.broadcast_to(ids[v][:, d : d + 1] == number, (TILE, cols))
+                    numerator += jnp.where(here, recv[v, d, 0].astype(F32), 0.0)
+                    denominator += jnp.where(here, recv[v, d, 1].astype(F32), 0.0)
+            gath[1 + my_block, q] = (numerator / jnp.maximum(denominator, 1.0)).astype(BF16)
+            return carry
+
+        if visits <= 4:
+            for q in range(visits):
+                one_patch(q, 0)
+        else:
+            lax.fori_loop(0, visits, one_patch, 0)
+        for v in range(visits):
+            @pl.when(me != v)
             def _():
-                for copy in ups:
-                    copy.start()
+                gather_copy(v, my_block).start()
+
+    if visits > blocks:
+        pl.when(me < blocks)(reduce)
+    else:
+        reduce()
 
     for copy in constants:
         copy.wait()
 
-    @pl.when(above)
-    def _():
-        for copy in downs:
-            copy.wait_recv()
-
-    @pl.when(below)
-    def _():
-        for copy in ups:
-            copy.wait_recv()
-
-    for t in order:
-        for k in range(1, visits):
-            gathers[t, k].wait_recv()
+    down = pltpu.make_async_remote_copy(
+        src_ref=gath.at[blocks], dst_ref=gath.at[0],
+        send_sem=halo_send.at[0], recv_sem=halo_recv.at[0],
+        device_id={"strip": lax.rem(strip + 1, strips)}, device_id_type=MESH,
+    )
+    up = pltpu.make_async_remote_copy(
+        src_ref=gath.at[1], dst_ref=gath.at[blocks + 1],
+        send_sem=halo_send.at[1], recv_sem=halo_recv.at[1],
+        device_id={"strip": lax.rem(strip + strips - 1, strips)}, device_id_type=MESH,
+    )
+    for t in [0, blocks - 1] + list(range(1, blocks - 1)):
+        r = block_of(t)
+
+        @pl.when(me != r)
+        def _():
+            gather_copy(r, t).wait_recv()
+
+        if t == 0:
+            pl.when(above)(up.start)
+        if t == blocks - 1:
+            pl.when(below)(down.start)
+    pl.when(above)(down.wait_recv)
+    pl.when(below)(up.wait_recv)
+    for t in range(blocks):
+        coadd_out[pl.ds(t * TILE, TILE), :] = gath[1 + t, me]
 
     top = BASES // 2 * cols
     vertical = tables[pl.ds(top, 3 * rows), pl.ds(0, rows + 2 * TILE)]
@@ -238,7 +265,7 @@
         return tables[pl.ds(c * cols, cols), pl.ds(0, cols)]
 
     for d in range(distinct):
-        template = gath[slots[d]]
+        template = jnp.concatenate([gath[i, slots[d]] for i in range(blocks + 2)], axis=0)
         smooth = nn(vertical, template).astype(BF16)
         planes = [None] * BASES
         for c in range(3):
@@ -326,18 +353,26 @@
     for d in range(distinct):
         mixers[d] = (mixer * member(d)).astype(BF16)
 
-    for copy in list(reduces.values()) + list(gathers.values()) + exchanges:
+    for copy in exchanges:
         copy.wait_send()
-
-    @pl.when(below)
-    def _():
-        for copy in downs:
-            copy.wait_send()
-
-    @pl.when(above)
-    def _():
-        for copy in ups:
-            copy.wait_send()
+    for r in range(blocks):
+        @pl.when(me != r)
+        def _():
+            for copy in reduce_copies(r, me):
+                copy.wait_send()
+
+    def gathered():
+        for v in range(visits):
+            @pl.when(me != v)
+            def _():
+                gather_copy(v, my_block).wait_send()
+
+    if visits > blocks:
+        pl.when(me < blocks)(gathered)
+    else:
+        gathered()
+    pl.when(below)(down.wait_send)
+    pl.when(above)(up.wait_send)
 
 
 def finish(coadd_in, image_v, basis, mixers, coadd_out, diff_out, diff_v, out_sem):
@@ -384,7 +419,6 @@
     vmem = pl.BlockSpec(memory_space=pltpu.VMEM)
     smem = pl.BlockSpec(memory_space=pltpu.SMEM)
     dma = pltpu.SemaphoreType.DMA
-    peers = max(1, visits - 1)
     cross = intersection.reshape(1, pieces)
     middle = pl.pallas_call(
         functools.partial(kernel, visits, strips, distinct),
@@ -401,21 +435,24 @@
             pltpu.VMEM(tables.shape, BF16),
             pltpu.VMEM((span, blocks * cols), BF16),
             pltpu.VMEM((span, blocks * cols), BF16),
-            pltpu.VMEM((blocks, visits, 2, TILE, cols), F32),
-            pltpu.VMEM((blocks, visits, 2, TILE, cols), BF16),
-            pltpu.VMEM((blocks, peers, 2, TILE, cols), BF16),
-            pltpu.VMEM((visits, rows + 2 * TILE, cols), BF16),
+            pltpu.VMEM((blocks, distinct, 2, TILE, cols), BF16),
+            pltpu.VMEM((visits, distinct, 2, TILE, cols), BF16),
+            pltpu.VMEM((1, 128), F32),
+            pltpu.VMEM((visits, 1, 128), F32),
+            pltpu.VMEM((blocks + 2, visits, TILE, cols), BF16),
             pltpu.VMEM((distinct, len(pairs) * TILE, blocks * cols), BF16),
             pltpu.VMEM((BASES * 8, 128), F32),
             pltpu.VMEM((max(1, strips - 1), BASES * 8, 128), F32),
             dma((2, blocks)),
             dma,
-            dma((blocks, peers)),
-            dma((blocks, peers)),
-            dma((blocks, peers)),
-            dma((blocks, peers)),
-            dma((2, visits)),
-            dma((2, visits)),
+            dma((blocks,)),
+            dma((visits,)),
+            dma((blocks,)),
+            dma((visits,)),
+            dma((visits,)),
+            dma((blocks,)),
+            dma((2,)),
+            dma((2,)),
             dma((max(1, strips - 1),)),
             dma((max(1, strips - 1),)),
         ],

time: 26.7 us -> 24.8 us (0.929)
  Pallas kernels: 25.3 us -> 23.3 us
    pallas_call x1, Pallas kernels: 24.1 us -> 22.1 us  [body(): pl.pallas_call(functools.partial(kernel, visits, strips, distinct), out_s...]
where the time goes in v3:
time: 24.8 us; the launch traced here: 24.6 us
  Pallas kernels  23.3 us (94%)
  local copies, waits for them, and re-layouts  0.66 us (3%)
  between operations  0.66 us (3%)
    pallas_call x1, Pallas kernels, body(): pl.pallas_call(functools.partial(kernel, visits, strips, distinct), out_s...  22.1 us
    pallas_call x1, Pallas kernels, body(): pl.pallas_call(finish, out_shape=(jax.ShapeDtypeStruct((1, 1, rows, cols)...  1.18 us
    unnamed x6, local copies, waits for them, and re-layouts  0.66 us

profile of v3, /device:TPU:0, one launch (start us, length us, event | category | flops | bytes accessed | tf_op | source)
XLA Modules:
  0.0 24.6 jit_solution(2270854058571771100)
XLA Ops:
  0.6 0.0 copy-start.2
  0.6 0.0 copy-start
  0.7 0.0 copy-start.1
  0.7 0.6 %copy-done.2 = s32[4]{0:T(128)S(1)} copy-done((s32[4]{0:T(128)S(1)}, s32[4]{0:T(128)}, u32[]{:S(2)}) %copy-start.2) | copy-done | bytes 40
  1.3 0.0 copy-done
  1.3 0.0 copy-done.1
  1.3 22.1 %coadd_solve.1 = (bf16[64,256]{1,0:T(8,128)(2,1)S(1)}, bf16[4,16,16,256]{3,2,1,0:T(8,128)(2,1)S(1)}, bf16[2,96,1024]{2,1,0:T(8,128)(2,1)S(1)}, bf16[2,256,192]{2,1,0:T(8,128)(2,1)S(1)}) custom-call(bf16[1,16,64,256]{3,2,1,0:T(8,128)(2,1)} %images.1, s32[1,16,64,256]{3,2,1,0:T(8,128)} %masks.1, bf16[1,16]{1,0:T(2,128)(2,1)S(1)} %copy-done.1, ...), custom_call_target="tpu_custom_call" | custom-call | tf_op jit(solution)/shard_map/coadd_solve/pallas_call | solution.py:423
  23.4 1.2 %difference.1 = (bf16[1,1,64,256]{3,2,1,0:T(8,128)(2,1)}, bf16[1,16,64,256]{3,2,1,0:T(8,128)(2,1)}) custom-call(bf16[64,256]{1,0:T(8,128)(2,1)S(1)} %get-tuple-element.6.coadd_in, bf16[4,16,16,256]{3,2,1,0:T(8,128)(2,1)S(1)} %get-tuple-element.7.image_v, bf16[2,96,1024]{2,1,0:T(8,128)(2,1)S(1)} %get-tuple-element.8.basis, ...), custom_call_target="tpu_custom_call" | custom-call | tf_op jit(solution)/shard_map/difference/pallas_call | solution.py:467
Async XLA Ops:
  0.6 0.7 %copy-start.2 = (s32[4]{0:T(128)S(1)}, s32[4]{0:T(128)}, u32[]{:S(2)}) copy-start(s32[4]{0:T(128)} %owner.1) | copy-start | bytes 52
  0.6 0.7 %copy-start = (s32[16,1]{0,1:T(1,128)S(1)}, s32[16,1]{0,1:T(1,128)}, u32[]{:S(2)}) copy-start(s32[16,1]{0,1:T(1,128)} %param.9) | copy-start | bytes 196
  0.7 0.7 %copy-start.1 = (bf16[1,16]{1,0:T(2,128)(2,1)S(1)}, bf16[1,16]{1,0:T(2,128)(2,1)}, u32[]{:S(2)}) copy-start(bf16[1,16]{1,0:T(2,128)(2,1)} %weight.1) | copy-start | bytes 100

commit v4 on v3

--- a/solution.py
+++ b/solution.py
@@ -73,6 +73,8 @@
     pieces, rows, cols = images.shape[1:]
     blocks = rows // TILE
     span = pieces * TILE
+    halves = send.shape[0]
+    lane = cols // halves
     order = [0] + ([blocks - 1] if blocks > 1 else []) + list(range(1, blocks - 1))
     me = lax.axis_index("visit")
     strip = lax.axis_index("strip")
@@ -144,7 +146,9 @@
         for part, value in enumerate((masked, usable)):
             total = nn(adder, value)
             for d in range(distinct):
-                send[t, d, part] = total[d * TILE : (d + 1) * TILE].astype(BF16)
+                block = total[d * TILE : (d + 1) * TILE].astype(BF16)
+                for h in range(halves):
+                    send[h, t, d, part] = block[:, h * lane : (h + 1) * lane]
     names = jnp.zeros((1, 128), jnp.int32)
     for d in range(distinct):
         names = names + jnp.where(iota((1, 128), 1) == d, slots[d], 0)
@@ -157,60 +161,63 @@
 
     my_block = me + 1 - 2 * lax.rem(me, 2) if blocks % 2 == 0 else me
 
-    def reduce_copies(r, source):
-        return (
-            pltpu.make_async_remote_copy(
-                src_ref=ids_own, dst_ref=ids.at[source],
-                send_sem=id_send.at[r], recv_sem=id_recv.at[source],
-                device_id={"visit": r}, device_id_type=MESH,
-            ),
-            pltpu.make_async_remote_copy(
-                src_ref=send.at[block_of(r)], dst_ref=recv.at[source],
-                send_sem=rs_send.at[r], recv_sem=rs_recv.at[source],
-                device_id={"visit": r}, device_id_type=MESH,
-            ),
+    def reduce_copies(h, r, source):
+        sums_copy = pltpu.make_async_remote_copy(
+            src_ref=send.at[h, block_of(r)], dst_ref=recv.at[h, source],
+            send_sem=rs_send.at[h, r], recv_sem=rs_recv.at[h, source],
+            device_id={"visit": r}, device_id_type=MESH,
         )
-
-    def gather_copy(v, block):
+        if h > 0:
+            return (sums_copy,)
+        names_copy = pltpu.make_async_remote_copy(
+            src_ref=ids_own, dst_ref=ids.at[source],
+            send_sem=id_send.at[r], recv_sem=id_recv.at[source],
+            device_id={"visit": r}, device_id_type=MESH,
+        )
+        return (names_copy, sums_copy)
+
+    def gather_copy(h, v, block):
         return pltpu.make_async_remote_copy(
-            src_ref=gath.at[1 + block], dst_ref=gath.at[1 + block],
-            send_sem=ag_send.at[v], recv_sem=ag_recv.at[block],
+            src_ref=gath.at[h, 1 + block], dst_ref=gath.at[h, 1 + block],
+            send_sem=ag_send.at[h, v], recv_sem=ag_recv.at[h, block],
             device_id={"visit": v}, device_id_type=MESH,
         )
 
-    for r in range(blocks):
-        @pl.when(me != r)
-        def _():
-            for copy in reduce_copies(r, me):
-                copy.start()
+    for h in range(halves):
+        for r in range(blocks):
+            @pl.when(me != r)
+            def _():
+                for copy in reduce_copies(h, r, me):
+                    copy.start()
 
     @pl.when(jnp.logical_not(above))
     def _():
-        gath[0] = jnp.zeros((visits, TILE, cols), BF16)
+        gath[:, 0] = jnp.zeros((halves, visits, TILE, lane), BF16)
 
     @pl.when(jnp.logical_not(below))
     def _():
-        gath[blocks + 1] = jnp.zeros((visits, TILE, cols), BF16)
-
-    def reduce():
-        recv[me] = send[my_block]
-        ids[me] = ids_own[...]
+        gath[:, blocks + 1] = jnp.zeros((halves, visits, TILE, lane), BF16)
+
+    def reduce(h):
+        recv[h, me] = send[h, my_block]
+        if h == 0:
+            ids[me] = ids_own[...]
         for v in range(visits):
             @pl.when(me != v)
             def _():
-                for copy in reduce_copies(0, v):
+                for copy in reduce_copies(h, 0, v):
                     copy.wait_recv()
 
         def one_patch(q, carry):
-            numerator = jnp.zeros((TILE, cols), F32)
-            denominator = jnp.zeros((TILE, cols), F32)
+            numerator = jnp.zeros((TILE, lane), F32)
+            denominator = jnp.zeros((TILE, lane), F32)
             number = lax.convert_element_type(q, F32)
             for v in range(visits):
                 for d in range(distinct):
-                    here = jnp.broadcast_to(ids[v][:, d : d + 1] == number, (TILE, cols))
-                    numerator += jnp.where(here, recv[v, d, 0].astype(F32), 0.0)
-                    denominator += jnp.where(here, recv[v, d, 1].astype(F32), 0.0)
-            gath[1 + my_block, q] = (numerator / jnp.maximum(denominator, 1.0)).astype(BF16)
+                    here = jnp.broadcast_to(ids[v][:, d : d + 1] == number, (TILE, lane))
+                    numerator += jnp.where(here, recv[h, v, d, 0].astype(F32), 0.0)
+                    denominator += jnp.where(here, recv[h, v, d, 1].astype(F32), 0.0)
+            gath[h, 1 + my_block, q] = (numerator / jnp.maximum(denominator, 1.0)).astype(BF16)
             return carry
 
         if visits <= 4:
@@ -221,41 +228,46 @@
         for v in range(visits):
             @pl.when(me != v)
             def _():
-                gather_copy(v, my_block).start()
-
-    if visits > blocks:
-        pl.when(me < blocks)(reduce)
-    else:
-        reduce()
+                gather_copy(h, v, my_block).start()
+
+    for h in range(halves):
+        if visits > blocks:
+            pl.when(me < blocks)(functools.partial(reduce, h))
+        else:
+            reduce(h)
 
     for copy in constants:
         copy.wait()
 
-    down = pltpu.make_async_remote_copy(
-        src_ref=gath.at[blocks], dst_ref=gath.at[0],
-        send_sem=halo_send.at[0], recv_sem=halo_recv.at[0],
+    downs = [pltpu.make_async_remote_copy(
+        src_ref=gath.at[h, blocks], dst_ref=gath.at[h, 0],
+        send_sem=halo_send.at[h, 0], recv_sem=halo_recv.at[h, 0],
         device_id={"strip": lax.rem(strip + 1, strips)}, device_id_type=MESH,
-    )
-    up = pltpu.make_async_remote_copy(
-        src_ref=gath.at[1], dst_ref=gath.at[blocks + 1],
-        send_sem=halo_send.at[1], recv_sem=halo_recv.at[1],
+    ) for h in range(halves)]
+    ups = [pltpu.make_async_remote_copy(
+        src_ref=gath.at[h, 1], dst_ref=gath.at[h, blocks + 1],
+        send_sem=halo_send.at[h, 1], recv_sem=halo_recv.at[h, 1],
         device_id={"strip": lax.rem(strip + strips - 1, strips)}, device_id_type=MESH,
-    )
-    for t in [0, blocks - 1] + list(range(1, blocks - 1)):
+    ) for h in range(halves)]
+    edges = sorted({0, blocks - 1})
+    inner = list(range(1, blocks - 1))
+    for h, t in [(h, t) for part in (edges, inner) for h in range(halves) for t in part]:
         r = block_of(t)
 
         @pl.when(me != r)
         def _():
-            gather_copy(r, t).wait_recv()
+            gather_copy(h, r, t).wait_recv()
 
         if t == 0:
-            pl.when(above)(up.start)
+            pl.when(above)(ups[h].start)
         if t == blocks - 1:
-            pl.when(below)(down.start)
-    pl.when(above)(down.wait_recv)
-    pl.when(below)(up.wait_recv)
-    for t in range(blocks):
-        coadd_out[pl.ds(t * TILE, TILE), :] = gath[1 + t, me]
+            pl.when(below)(downs[h].start)
+    for h in range(halves):
+        pl.when(above)(downs[h].wait_recv)
+        pl.when(below)(ups[h].wait_recv)
+    for h in range(halves):
+        for t in range(blocks):
+            coadd_out[pl.ds(t * TILE, TILE), pl.ds(h * lane, lane)] = gath[h, 1 + t, me]
 
     top = BASES // 2 * cols
     vertical = tables[pl.ds(top, 3 * rows), pl.ds(0, rows + 2 * TILE)]
@@ -265,7 +277,10 @@
         return tables[pl.ds(c * cols, cols), pl.ds(0, cols)]
 
     for d in range(distinct):
-        template = jnp.concatenate([gath[i, slots[d]] for i in range(blocks + 2)], axis=0)
+        template = jnp.concatenate([
+            jnp.concatenate([gath[h, i, slots[d]] for i in range(blocks + 2)], axis=0)
+            for h in range(halves)
+        ], axis=1)
         smooth = nn(vertical, template).astype(BF16)
         planes = [None] * BASES
         for c in range(3):
@@ -355,24 +370,25 @@
 
     for copy in exchanges:
         copy.wait_send()
-    for r in range(blocks):
-        @pl.when(me != r)
-        def _():
-            for copy in reduce_copies(r, me):
-                copy.wait_send()
-
-    def gathered():
+    def gathered(h):
         for v in range(visits):
             @pl.when(me != v)
             def _():
-                gather_copy(v, my_block).wait_send()
-
-    if visits > blocks:
-        pl.when(me < blocks)(gathered)
-    else:
-        gathered()
-    pl.when(below)(down.wait_send)
-    pl.when(above)(up.wait_send)
+                gather_copy(h, v, my_block).wait_send()
+
+    for h in range(halves):
+        for r in range(blocks):
+            @pl.when(me != r)
+            def _():
+                for copy in reduce_copies(h, r, me):
+                    copy.wait_send()
+
+        if visits > blocks:
+            pl.when(me < blocks)(functools.partial(gathered, h))
+        else:
+            gathered(h)
+        pl.when(below)(downs[h].wait_send)
+        pl.when(above)(ups[h].wait_send)
 
 
 def finish(coadd_in, image_v, basis, mixers, coadd_out, diff_out, diff_v, out_sem):
@@ -403,6 +419,8 @@
     blocks = rows // TILE
     distinct = max(1, patch_owner.shape[0] // 2)
     span = pieces * TILE
+    halves = max(1, cols // 128)
+    lane = cols // halves
     taps = kernel_taps()
     collect = gather_matrix()
     width = max(collect.shape[1], cols, rows + 2 * TILE)
@@ -435,24 +453,24 @@
             pltpu.VMEM(tables.shape, BF16),
             pltpu.VMEM((span, blocks * cols), BF16),
             pltpu.VMEM((span, blocks * cols), BF16),
-            pltpu.VMEM((blocks, distinct, 2, TILE, cols), BF16),
-            pltpu.VMEM((visits, distinct, 2, TILE, cols), BF16),
+            pltpu.VMEM((halves, blocks, distinct, 2, TILE, lane), BF16),
+            pltpu.VMEM((halves, visits, distinct, 2, TILE, lane), BF16),
             pltpu.VMEM((1, 128), F32),
             pltpu.VMEM((visits, 1, 128), F32),
-            pltpu.VMEM((blocks + 2, visits, TILE, cols), BF16),
+            pltpu.VMEM((halves, blocks + 2, visits, TILE, lane), BF16),
             pltpu.VMEM((distinct, len(pairs) * TILE, blocks * cols), BF16),
             pltpu.VMEM((BASES * 8, 128), F32),
             pltpu.VMEM((max(1, strips - 1), BASES * 8, 128), F32),
             dma((2, blocks)),
             dma,
+            dma((halves, blocks)),
+            dma((halves, visits)),
             dma((blocks,)),
             dma((visits,)),
-            dma((blocks,)),
-            dma((visits,)),
-            dma((visits,)),
-            dma((blocks,)),
-            dma((2,)),
-            dma((2,)),
+            dma((halves, visits)),
+            dma((halves, blocks)),
+            dma((halves, 2)),
+            dma((halves, 2)),
             dma((max(1, strips - 1),)),
             dma((max(1, strips - 1),)),
         ],

time: 24.8 us -> 24.8 us (level)
  no operation moved by 1% of the time
where the time goes in v4:
time: 24.8 us; the launch traced here: 24.6 us
  Pallas kernels  23.3 us (94%)
  local copies, waits for them, and re-layouts  0.66 us (3%)
  between operations  0.66 us (3%)
    pallas_call x1, Pallas kernels, body(): pl.pallas_call(functools.partial(kernel, visits, strips, distinct), out_s...  22.1 us
    pallas_call x1, Pallas kernels, body(): pl.pallas_call(finish, out_shape=(jax.ShapeDtypeStruct((1, 1, rows, cols)...  1.18 us
    unnamed x6, local copies, waits for them, and re-layouts  0.66 us

profile of v4, /device:TPU:0, one launch (start us, length us, event | category | flops | bytes accessed | tf_op | source)
XLA Modules:
  0.0 24.6 jit_solution(6265011984141327253)
XLA Ops:
  0.6 0.0 copy-start.2
  0.6 0.0 copy-start
  0.7 0.0 copy-start.1
  0.7 0.6 %copy-done.2 = s32[4]{0:T(128)S(1)} copy-done((s32[4]{0:T(128)S(1)}, s32[4]{0:T(128)}, u32[]{:S(2)}) %copy-start.2) | copy-done | bytes 40
  1.3 0.0 copy-done
  1.3 0.0 copy-done.1
  1.3 22.1 %coadd_solve.1 = (bf16[64,256]{1,0:T(8,128)(2,1)S(1)}, bf16[4,16,16,256]{3,2,1,0:T(8,128)(2,1)S(1)}, bf16[2,96,1024]{2,1,0:T(8,128)(2,1)S(1)}, bf16[2,256,192]{2,1,0:T(8,128)(2,1)S(1)}) custom-call(bf16[1,16,64,256]{3,2,1,0:T(8,128)(2,1)} %images.1, s32[1,16,64,256]{3,2,1,0:T(8,128)} %masks.1, bf16[1,16]{1,0:T(2,128)(2,1)S(1)} %copy-done.1, ...), custom_call_target="tpu_custom_call" | custom-call | tf_op jit(solution)/shard_map/coadd_solve/pallas_call | solution.py:441
  23.4 1.2 %difference.1 = (bf16[1,1,64,256]{3,2,1,0:T(8,128)(2,1)}, bf16[1,16,64,256]{3,2,1,0:T(8,128)(2,1)}) custom-call(bf16[64,256]{1,0:T(8,128)(2,1)S(1)} %get-tuple-element.6.coadd_in, bf16[4,16,16,256]{3,2,1,0:T(8,128)(2,1)S(1)} %get-tuple-element.7.image_v, bf16[2,96,1024]{2,1,0:T(8,128)(2,1)S(1)} %get-tuple-element.8.basis, ...), custom_call_target="tpu_custom_call" | custom-call | tf_op jit(solution)/shard_map/difference/pallas_call | solution.py:485
Async XLA Ops:
  0.6 0.7 %copy-start.2 = (s32[4]{0:T(128)S(1)}, s32[4]{0:T(128)}, u32[]{:S(2)}) copy-start(s32[4]{0:T(128)} %owner.1) | copy-start | bytes 52
  0.6 0.7 %copy-start = (s32[16,1]{0,1:T(1,128)S(1)}, s32[16,1]{0,1:T(1,128)}, u32[]{:S(2)}) copy-start(s32[16,1]{0,1:T(1,128)} %param.9) | copy-start | bytes 196
  0.7 0.7 %copy-start.1 = (bf16[1,16]{1,0:T(2,128)(2,1)S(1)}, bf16[1,16]{1,0:T(2,128)(2,1)}, u32[]{:S(2)}) copy-start(bf16[1,16]{1,0:T(2,128)(2,1)} %weight.1) | copy-start | bytes 100

commit v5 on v3

--- a/solution.py
+++ b/solution.py
@@ -178,11 +178,13 @@
             device_id={"visit": v}, device_id_type=MESH,
         )
 
-    for r in range(blocks):
-        @pl.when(me != r)
-        def _():
-            for copy in reduce_copies(r, me):
-                copy.start()
+    low = me * 2 < visits
+    for side, targets in ((low, range(blocks - 1, -1, -1)), (jnp.logical_not(low), range(blocks))):
+        for r in targets:
+            @pl.when(jnp.logical_and(side, me != r))
+            def _():
+                for copy in reduce_copies(r, me):
+                    copy.start()
 
     @pl.when(jnp.logical_not(above))
     def _():
@@ -218,10 +220,13 @@
                 one_patch(q, 0)
         else:
             lax.fori_loop(0, visits, one_patch, 0)
-        for v in range(visits):
-            @pl.when(me != v)
-            def _():
-                gather_copy(v, my_block).start()
+        for side, targets in (
+            (low, range(visits - 1, -1, -1)), (jnp.logical_not(low), range(visits))
+        ):
+            for v in targets:
+                @pl.when(jnp.logical_and(side, me != v))
+                def _():
+                    gather_copy(v, my_block).start()
 
     if visits > blocks:
         pl.when(me < blocks)(reduce)

time: 24.8 us -> 25 us (level)
  no operation moved by 1% of the time
where the time goes in v5:
time: 25 us; the launch traced here: 24.8 us
  Pallas kernels  23.5 us (94%)
  local copies, waits for them, and re-layouts  0.66 us (3%)
  between operations  0.66 us (3%)
    pallas_call x1, Pallas kernels, body(): pl.pallas_call(functools.partial(kernel, visits, strips, distinct), out_s...  22.3 us
    pallas_call x1, Pallas kernels, body(): pl.pallas_call(finish, out_shape=(jax.ShapeDtypeStruct((1, 1, rows, cols)...  1.18 us
    unnamed x6, local copies, waits for them, and re-layouts  0.66 us

profile of v5, /device:TPU:0, one launch (start us, length us, event | category | flops | bytes accessed | tf_op | source)
XLA Modules:
  0.0 24.8 jit_solution(8004118424015872540)
XLA Ops:
  0.6 0.0 copy-start.2
  0.6 0.0 copy-start
  0.7 0.0 copy-start.1
  0.7 0.6 %copy-done.2 = s32[4]{0:T(128)S(1)} copy-done((s32[4]{0:T(128)S(1)}, s32[4]{0:T(128)}, u32[]{:S(2)}) %copy-start.2) | copy-done | bytes 40
  1.3 0.0 copy-done
  1.3 0.0 copy-done.1
  1.3 22.3 %coadd_solve.1 = (bf16[64,256]{1,0:T(8,128)(2,1)S(1)}, bf16[4,16,16,256]{3,2,1,0:T(8,128)(2,1)S(1)}, bf16[2,96,1024]{2,1,0:T(8,128)(2,1)S(1)}, bf16[2,256,192]{2,1,0:T(8,128)(2,1)S(1)}) custom-call(bf16[1,16,64,256]{3,2,1,0:T(8,128)(2,1)} %images.1, s32[1,16,64,256]{3,2,1,0:T(8,128)} %masks.1, bf16[1,16]{1,0:T(2,128)(2,1)S(1)} %copy-done.1, ...), custom_call_target="tpu_custom_call" | custom-call | tf_op jit(solution)/shard_map/coadd_solve/pallas_call | solution.py:428
  23.7 1.2 %difference.1 = (bf16[1,1,64,256]{3,2,1,0:T(8,128)(2,1)}, bf16[1,16,64,256]{3,2,1,0:T(8,128)(2,1)}) custom-call(bf16[64,256]{1,0:T(8,128)(2,1)S(1)} %get-tuple-element.6.coadd_in, bf16[4,16,16,256]{3,2,1,0:T(8,128)(2,1)S(1)} %get-tuple-element.7.image_v, bf16[2,96,1024]{2,1,0:T(8,128)(2,1)S(1)} %get-tuple-element.8.basis, ...), custom_call_target="tpu_custom_call" | custom-call | tf_op jit(solution)/shard_map/difference/pallas_call | solution.py:472
Async XLA Ops:
  0.6 0.7 %copy-start.2 = (s32[4]{0:T(128)S(1)}, s32[4]{0:T(128)}, u32[]{:S(2)}) copy-start(s32[4]{0:T(128)} %owner.1) | copy-start | bytes 52
  0.6 0.7 %copy-start = (s32[16,1]{0,1:T(1,128)S(1)}, s32[16,1]{0,1:T(1,128)}, u32[]{:S(2)}) copy-start(s32[16,1]{0,1:T(1,128)} %param.9) | copy-start | bytes 196
  0.7 0.7 %copy-start.1 = (bf16[1,16]{1,0:T(2,128)(2,1)S(1)}, bf16[1,16]{1,0:T(2,128)(2,1)}, u32[]{:S(2)}) copy-start(bf16[1,16]{1,0:T(2,128)(2,1)} %weight.1) | copy-start | bytes 100
